TPU v7x, 256 devices: a whole 4x4x8 slice. The times are simulated.
256 devices in a mesh: rep: 8 (over x, z_hi), seq: 4 (over y), tp: 8 (over z_lo, core).
Axes of the slice: x: 4, y: 4, z: 8 (z_hi: 2, z_lo: 4; z = z_hi * 4 + z_lo), core: 2. Of those that a mesh axis runs over, the one named last changes fastest.
Arguments:
- hidden_in: bfloat16 [32768, 1536], P(('rep', 'seq', 'tp')), may hold values from -3 to 3
- routes: int32 [32768, 4], P(('rep', 'seq', 'tp')), may hold values from 0 to 31, all different within a row; in each aligned block of 128 rows (0 to 127, 128 to 255, ...) at most 24 rows name the same one
- prefix_len: int32 [8], replicated, may hold values from 256 to 2048, as said below
- cache: bfloat16 [8, 2, 2048, 256], P(None, None, ('rep', 'seq')), may hold values from -400 to 400, as said below
- attn_gain: float32 [1536], replicated, may hold values from 0.1 to 1.9
- w_query: bfloat16 [1536, 1024], P(None, 'tp'), may hold values from -0.375 to 0.375
- w_keyval: bfloat16 [2, 1536, 256], replicated, may hold values from -0.15625 to 0.15625
- w_out: bfloat16 [1024, 1536], P('tp'), may hold values from -0.375 to 0.375
- moe_gain: float32 [1536], replicated, may hold values from 0.1 to 1.9
- w_router: bfloat16 [1536, 32], replicated, may hold values from -0.15625 to 0.15625
- expert_in: bfloat16 [32, 1536, 1536], P(('seq', 'tp')), may hold values from -0.15625 to 0.15625
- expert_out: bfloat16 [32, 768, 1536], P(('seq', 'tp')), may hold values from -0.875 to 0.875
Outputs:
- hidden_out: bfloat16 [32768, 1536], P(('rep', 'seq', 'tp'))
- new_cache: bfloat16 [32768, 512], P(('rep', 'seq'), 'tp')
Inputs may be any that keep to these rules, and one draw needn't show every extreme that they name: `routes`: each row names 4 different experts; within the rows of one device (aligned blocks of 128 rows) no expert is named by more than 24 rows. prefix_len[r] cached positions (0 to prefix_len[r] - 1) of request r are valid; some request has 2048. cache[r, g, p, 0:128] is a key, cache[r, g, p, 128:] a value.
All inputs are finite; a program needn't handle non-finite values.
Results may differ from a plain program's by a relative error of at most 0.029.
The roundings to bfloat16 on the way count: a program that leaves them out, or rounds other values in their place, can miss the bound.
Values may be sent and summed in bfloat16 or wider, within the bound.
No kernel may reach another device: no remote copies, remote signals or barrier semaphores. Data moves between devices by JAX's collectives and lax.ppermute only.
A program may use at most 64 MiB of HBM per device.

v0:
```python
import jax
import jax.numpy as jnp
from jax import lax
from jax.sharding import PartitionSpec as P

CAP = 24
epsilon = 1e-06
masked_score = -1e30


def rms_scale(rows, gain):
    values = rows.astype(jnp.float32)
    inverse = lax.rsqrt(jnp.mean(values * values, axis=-1, keepdims=True) + epsilon)
    return (values * inverse * gain).astype(jnp.bfloat16)


def attend(state, query_rows, block, visible, scale):
    best, total, summed = state
    head_dim = block.shape[1] // 2
    scores = (
        lax.dot_general(
            query_rows,
            block[:, :head_dim],
            (((1,), (1,)), ((), ())),
            preferred_element_type=jnp.float32,
        )
        * scale
    )
    scores = jnp.where(visible, scores, masked_score)
    new_best = jnp.maximum(best, jnp.max(scores, axis=1))
    weights = jnp.where(visible, jnp.exp(scores - new_best[:, None]), 0.0)
    factor = jnp.exp(best - new_best)
    total = total * factor + jnp.sum(weights, axis=1)
    summed = summed * factor[:, None] + jnp.dot(
        weights.astype(jnp.bfloat16), block[:, head_dim:], preferred_element_type=jnp.float32
    )
    return (new_best, total, summed)


def body(
    hidden_in,
    routes,
    prefix_len,
    cache,
    attn_gain,
    w_query,
    w_keyval,
    w_out,
    moe_gain,
    w_router,
    expert_in,
    expert_out,
):
    tp_count = lax.axis_size("tp")
    seq_count = lax.axis_size("seq")
    rep_count = lax.axis_size("rep")
    tp_index = lax.axis_index("tp")
    seq_index = lax.axis_index("seq")
    rep_index = lax.axis_index("rep")
    rows_dev, width = hidden_in.shape
    kv_heads = w_keyval.shape[0]
    pair_cols = w_keyval.shape[2]
    head_dim = pair_cols // 2
    query_cols = w_query.shape[1]
    heads_dev = query_cols // head_dim
    piece_len = rows_dev * tp_count
    scale = 1.0 / float(head_dim) ** 0.5
    kv_index = tp_index // (tp_count // kv_heads)
    normed = rms_scale(hidden_in, attn_gain)
    head_weight = lax.dynamic_index_in_dim(w_keyval, kv_index, 0, keepdims=False)
    joined = jnp.concatenate([w_query, head_weight], axis=1)
    projected = jnp.dot(
        lax.all_gather(normed, "tp", axis=0, tiled=True), joined, preferred_element_type=jnp.float32
    ).astype(jnp.bfloat16)
    count_rows = piece_len * heads_dev
    query_rows = projected[:, :query_cols]
    fresh = projected[:, query_cols:]
    col_width = kv_heads * pair_cols // tp_count
    new_cache = lax.dynamic_slice_in_dim(fresh, tp_index * col_width % pair_cols, col_width, 1)
    own_pages = lax.dynamic_index_in_dim(cache, kv_index, 1, keepdims=True)
    fetched = lax.all_to_all(own_pages, "rep", split_axis=0, concat_axis=2, tiled=True)
    page_rows = fetched.shape[2]
    pages = fetched.reshape(page_rows, pair_cols)
    page_len = page_rows // rep_count
    length = lax.dynamic_index_in_dim(prefix_len, rep_index, 0, keepdims=False)
    row_ids = jnp.arange(page_rows, dtype=jnp.int32)

    def page_visible(source):
        position = (row_ids // page_len * seq_count + source) * page_len + row_ids % page_len
        return (position < length)[None, :]

    def fresh_visible(source, query_piece):
        token = jnp.arange(count_rows, dtype=jnp.int32) // heads_dev + query_piece * piece_len
        key_pos = source * piece_len + jnp.arange(piece_len, dtype=jnp.int32)
        return key_pos[None, :] <= token[:, None]

    start_state = (
        jnp.full((count_rows,), masked_score, jnp.float32),
        jnp.zeros((count_rows,), jnp.float32),
        jnp.zeros((count_rows, head_dim), jnp.float32),
    )
    shard_rows = page_rows + piece_len
    local_keys = jnp.concatenate([pages, fresh], axis=0)

    def fold_shard(state, shard, source):
        state = attend(state, query_rows, shard[:page_rows], page_visible(source), scale)

        def with_fresh(inner):
            return attend(
                inner, query_rows, shard[page_rows:], fresh_visible(source, seq_index), scale
            )

        return lax.cond(source <= seq_index, with_fresh, lambda inner: inner, state)

    state = start_state
    gathered = lax.all_gather(local_keys, "seq", axis=0, tiled=True)
    count = gathered.shape[0] // shard_rows
    shards = gathered.reshape(count, shard_rows, pair_cols)

    def advance(inner, item):
        offset, shard = item
        return (fold_shard(inner, shard, offset), None)

    state, _ = lax.scan(advance, state, (jnp.arange(count, dtype=jnp.int32), shards))
    best, total, summed = state
    attended = (summed / total[:, None]).astype(jnp.bfloat16)
    rows = attended
    head_total = lax.psum_scatter(
        jnp.dot(rows, w_out, preferred_element_type=jnp.float32),
        "tp",
        scatter_dimension=0,
        tiled=True,
    )
    mid = (hidden_in.astype(jnp.float32) + head_total).astype(jnp.bfloat16)
    normed_moe = rms_scale(mid, moe_gain)
    experts_all = w_router.shape[1]
    top = routes.shape[1]
    expert_ids = jnp.arange(experts_all, dtype=jnp.int32)
    logits = jnp.dot(normed_moe, w_router, preferred_element_type=jnp.float32)
    matches = routes[:, :, None] == expert_ids[None, None, :]
    chosen = jnp.sum(jnp.where(matches, logits[:, None, :], 0.0), axis=2)
    raised = jnp.exp(chosen)
    gates = raised / jnp.sum(raised, axis=1, keepdims=True)
    flat_routes = routes.reshape(rows_dev * top)
    onehot = (flat_routes[:, None] == expert_ids[None, :]).astype(jnp.int32)
    before = jnp.cumsum(onehot, axis=0) - onehot
    slot = jnp.sum(before * onehot, axis=1)
    target = flat_routes * CAP + slot
    outgoing = (
        jnp.zeros((experts_all * CAP, width), jnp.bfloat16)
        .at[target]
        .set(jnp.repeat(normed_moe, top, axis=0))
    )
    group_count = seq_count * tp_count
    local_experts = expert_in.shape[0]
    inner_dim = expert_out.shape[1]
    arrived = lax.all_to_all(
        outgoing.reshape(group_count, local_experts, CAP, width),
        ("seq", "tp"),
        split_axis=0,
        concat_axis=0,
        tiled=True,
    )
    rows = arrived[:, 0].reshape(-1, width)
    inner = jnp.dot(rows, expert_in[0], preferred_element_type=jnp.float32)
    active = (jnp.maximum(inner[:, :inner_dim], 0.0) * inner[:, inner_dim:]).astype(jnp.bfloat16)
    output = jnp.dot(active, expert_out[0], preferred_element_type=jnp.float32).astype(jnp.bfloat16)
    results = [output.reshape(arrived.shape[0], arrived.shape[2], width)]
    returned = lax.all_to_all(
        jnp.stack(results, axis=1), ("seq", "tp"), split_axis=0, concat_axis=0, tiled=True
    )
    picked = returned.reshape(experts_all * CAP, width)[target].reshape(rows_dev, top, width)
    mixed = jnp.sum(gates[:, :, None] * picked.astype(jnp.float32), axis=1)
    hidden_out = (mid.astype(jnp.float32) + mixed).astype(jnp.bfloat16)
    return (hidden_out, new_cache)


def solution(mesh):
    placed = (
        P(("rep", "seq", "tp"), None),
        P(("rep", "seq", "tp"), None),
        P(),
        P(None, None, ("rep", "seq"), None),
        P(),
        P(None, "tp"),
        P(),
        P("tp", None),
        P(),
        P(),
        P(("seq", "tp"), None, None),
        P(("seq", "tp"), None, None),
    )
    return jax.shard_map(
        body,
        mesh=mesh,
        in_specs=placed,
        out_specs=(P(("rep", "seq", "tp"), None), P(("rep", "seq"), "tp")),
        check_vma=False,
    )
```

profile of v0, /device:TPU:1, one launch (start us, length us, event | category | flops | bytes accessed | tf_op | source)
XLA Modules:
  0.0 418.8 jit_solution(9488731846069213498)
XLA Ops:
  12.2 11.5 %all-to-all-start = ((bf16[8,1,64,256]{3,2,1,0:T(8,128)(2,1)}), bf16[8,1,64,256]{3,2,1,0:T(8,128)(2,1)S(1)}, u32[]{:S(2)}, u32[]{:S(2)}) async-start(bf16[8,1,64,256]{3,2,1,0:T(8,128)(2,1)} %constant_dynamic-slice_fusion.2), calls=%async_computation | async-start | bytes 524288 | tf_op jit(solution)/shard_map/all_to_all | solution.py:81
  25.8 8.2 %all-to-all-done = bf16[8,1,64,256]{3,2,1,0:T(8,128)(2,1)S(1)} async-done(((bf16[8,1,64,256]{3,2,1,0:T(8,128)(2,1)}), bf16[8,1,64,256]{3,2,1,0:T(8,128)(2,1)S(1)}, u32[]{:S(2)}, u32[]{:S(2)}) %all-to-all-start) | async-done | bytes 262176 | tf_op jit(solution)/shard_map/all_to_all | solution.py:81
  34.2 26.8 %all-gather.3.cloned.1.call-done = bf16[1024,1536]{1,0:T(8,128)(2,1)} async-done(((bf16[128,1536]{1,0:T(8,128)(2,1)}), bf16[1024,1536]{1,0:T(8,128)(2,1)}) %all-gather.3.cloned.1.call-update) | async-done | bytes 3145744 | tf_op jit(solution)/shard_map/all_gather | solution.py:73
  61.0 3.5 convolution_convert_fusion.1
  69.2 41.3 %all-gather.5.cloned.1.call-done = bf16[6144,256]{0,1:T(8,128)(2,1)} async-done(((bf16[1536,256]{0,1:T(8,128)(2,1)}), bf16[6144,256]{0,1:T(8,128)(2,1)}) %all-gather.5.cloned.1.call-update) | async-done | bytes 3145744 | tf_op jit(solution)/shard_map/all_gather | solution.py:116
  110.6 4.6 %copy.48 = bf16[6144,256]{1,0:T(8,128)(2,1)} copy(bf16[6144,256]{0,1:T(8,128)(2,1)} %all-gather.5.cloned.1.call-done) | data formatting | bytes 6291456
  116.0 39.8 %while.20 = (s32[]{:T(128)}, f32[1024]{0:T(1024)S(1)}, f32[1024]{0:T(1024)S(1)}, f32[1024,128]{1,0:T(8,128)}, s32[4]{0:T(128)S(1)}, /*index=5*/s32[]{:T(128)}, s...) while((s32[]{:T(128)}, f32[1024]{0:T(1024)S(1)}, ...), condition=%wide.region_8.9_spmd.clone.clone, body=%wide.region_1.8_spmd.clone.clone.sunk | while | flops 829438464 | bytes 24546600 | solution.py:124
  121.7 2.7 convolution_add_fusion.2
  124.4 6.2 %conditional.4 = ((f32[1024]{0:T(1024)S(1)}, f32[1024]{0:T(1024)S(1)}, f32[1024,128]{1,0:T(8,128)})) conditional(s32[]{:T(128)} %convert_element_type.129, (f32[1024]{0:T(1024)S(1)}, f32[1024]{0:T(1024)S(1)}, f32[1024,128]{1,0:T(8,128)}) %tuple.70, (s32[]{:T(128)}, s32[]{:T(128)}, bf16[1,1536,256]{2,1,0:T(8,128)(2,1)S(1)}, ...), branch_computations={%region_4.4_spmd, %region_5.7_spmd} | conditional | flops 553914368 | bytes 14516288 | solution.py:113
  127.4 3.3 fusion.13
  136.3 2.7 convolution_add_fusion.2
  144.7 2.7 convolution_add_fusion.2
  155.8 4.8 %fusion.65 = f32[1024,1536]{1,0:T(8,128)} fusion(bf16[128,1536]{1,0:T(8,128)(2,1)} %param.23, f32[1024,128]{1,0:T(8,128)} %get-tuple-element.277, f32[1024]{0:T(1024)S(1)} %get-tuple-element.278), kind=kOutput, calls=%fused_computation.89 | convolution fusion | flops 402915328 | bytes 7213056 | tf_op jit(solution)/shard_map/dot_general | solution.py:129
  163.5 87.9 %reduce-scatter.2.cloned.1.call-done = f32[128,1536]{1,0:T(8,128)} async-done(((f32[1024,1536]{1,0:T(8,128)}), f32[128,1536]{1,0:T(8,128)}) %reduce-scatter.2.cloned.1.call-update) | async-done | bytes 786448 | tf_op jit(solution)/shard_map/reduce_scatter | solution.py:128
  254.5 3.7 reshape.208
  258.2 5.5 %scatter_custom_fusion = bf16[768,1536]{1,0:T(8,128)(2,1)} fusion(s32[512]{0:T(512)S(1)} %bitcast.64, bf16[512,1536]{1,0:T(8,128)(2,1)} %reshape.208, bf16[]{:T(256)} %constant.204.clone.1), kind=kCustom, calls=%fused_computation.76 | custom fusion | bytes 2359808 | tf_op jit(solution)/shard_map/scatter | solution.py:152
  263.8 63.9 %all_to_all.19 = bf16[32,1,24,1536]{3,2,1,0:T(8,128)(2,1)S(1)} all-to-all(bf16[32,1,24,1536]{3,2,1,0:T(8,128)(2,1)} %bitcast.60), channel_id=1, replica_groups=mesh['rep'=8,'seq'=4,'tp'=8] {'seq','tp'}, dimensions={0} | all-to-all | bytes 4718592 | tf_op jit(solution)/shard_map/all_to_all | solution.py:157
  327.7 5.7 %fusion.46 = f32[768,1536]{1,0:T(8,128)S(1)} fusion(bf16[768,1536]{1,0:T(8,128)(2,1)S(1)} %bitcast.62, bf16[1,1536,1536]{2,1,0:T(8,128)(2,1)} %param.26), kind=kOutput, calls=%fused_computation.57 | convolution fusion | flops 3623878656 | bytes 11796480 | tf_op jit(solution)/shard_map/dot_general | solution.py:165
  333.4 3.4 convolution_convert_fusion
  336.7 4.7 %all-to-all-start.2 = ((bf16[32,1,24,1536]{3,2,1,0:T(8,128)(2,1)}), bf16[32,1,24,1536]{3,2,1,0:T(8,128)(2,1)}, u32[]{:S(2)}, u32[]{:S(2)}) async-start(bf16[32,1,24,1536]{3,2,1,0:T(8,128)(2,1)} %bitcast.61), calls=%async_computation.3 | async-start | bytes 4718592 | tf_op jit(solution)/shard_map/all_to_all | solution.py:169
  343.5 53.2 %all-to-all-done.2 = bf16[32,1,24,1536]{3,2,1,0:T(8,128)(2,1)} async-done(((bf16[32,1,24,1536]{3,2,1,0:T(8,128)(2,1)}), bf16[32,1,24,1536]{3,2,1,0:T(8,128)(2,1)}, u32[]{:S(2)}, u32[]{:S(2)}) %all-to-all-start.2) | async-done | bytes 2359328 | tf_op jit(solution)/shard_map/all_to_all | solution.py:169
  396.7 6.4 %gather_fusion = bf16[512,1536]{1,0:T(8,128)(2,1)} fusion(bf16[768,1536]{1,0:T(8,128)(2,1)} %bitcast.14, s32[1024]{0:T(1024)S(1)} %pad_clamp_fusion), kind=kCustom, calls=%fused_computation | custom fusion | bytes 3147776 | tf_op jit(solution)/shard_map/gather | solution.py:172
  403.1 4.2 %reshape.195 = f32[128,4,1536]{2,1,0:T(4,128)} reshape(bf16[512,1536]{1,0:T(8,128)(2,1)} %gather_fusion) | data formatting | bytes 4718592 | tf_op jit(solution)/shard_map/convert_element_type | solution.py:173
  407.3 4.2 multiply_reduce_fusion
  (114 shorter events, 46.8 us)
Async XLA Ops:
  7.2 326.2 %copy-start = (bf16[1,768,1536]{2,1,0:T(8,128)(2,1)S(1)}, bf16[1,768,1536]{2,1,0:T(8,128)(2,1)}, u32[]{:S(2)}) copy-start(bf16[1,768,1536]{2,1,0:T(8,128)(2,1)} %param.27) | copy-start | bytes 7077892
  7.2 53.8 %copy-start.7 = (bf16[1536,128]{1,0:T(8,128)(2,1)S(1)}, bf16[1536,128]{1,0:T(8,128)(2,1)}, u32[]{:S(2)}) copy-start(bf16[1536,128]{1,0:T(8,128)(2,1)} %param.21) | copy-start | bytes 1179652
  7.2 53.8 %all-gather.3.cloned.1.call-start = ((), (), s32[]{:S(2)}) async-start(), calls=%async_computation.4 | async-start | bytes 3538944 | tf_op jit(solution)/shard_map/all_gather | solution.py:73
  12.2 21.8 %all-to-all-start = ((bf16[8,1,64,256]{3,2,1,0:T(8,128)(2,1)}), bf16[8,1,64,256]{3,2,1,0:T(8,128)(2,1)S(1)}, u32[]{:S(2)}, u32[]{:S(2)}) async-start(bf16[8,1,64,256]{3,2,1,0:T(8,128)(2,1)} %constant_dynamic-slice_fusion.2), calls=%async_computation | async-start | bytes 524288 | tf_op jit(solution)/shard_map/all_to_all | solution.py:81
  23.7 86.9 %all-gather.5.cloned.1.call-start = ((), (), s32[]{:S(2)}) async-start(), calls=%async_computation.5 | async-start | bytes 3932160 | tf_op jit(solution)/shard_map/all_gather | solution.py:116
  64.5 0.9 copy-start.3
  65.4 2.1 copy-start.8
  65.4 0.8 copy-start.2
  67.2 184.3 %reduce-scatter.2.cloned.1.call-start = ((), (), s32[]{:S(2)}) async-start(), calls=%async_computation.6 | async-start | bytes 7077888 | tf_op jit(solution)/shard_map/reduce_scatter | solution.py:128
  160.7 0.7 copy-start.5
  160.7 90.8 %copy-start.1 = (bf16[128,1536]{1,0:T(8,128)(2,1)S(1)}, bf16[128,1536]{1,0:T(8,128)(2,1)}, u32[]{:S(2)}) copy-start(bf16[128,1536]{1,0:T(8,128)(2,1)} %param.16) | copy-start | bytes 1179652
  160.7 92.1 %copy-start.6 = (f32[1536]{0:T(1024)S(1)}, f32[1536]{0:T(1024)}, u32[]{:S(2)}) copy-start(f32[1536]{0:T(1024)} %param.24) | copy-start | bytes 18436
  336.7 6.3 %copy-start.4 = (bf16[1536,32]{0,1:T(8,128)(2,1)S(1)}, bf16[1536,32]{0,1:T(8,128)(2,1)}, u32[]{:S(2)}) copy-start(bf16[1536,32]{0,1:T(8,128)(2,1)} %param.25) | copy-start | bytes 294916
  336.7 60.0 %all-to-all-start.2 = ((bf16[32,1,24,1536]{3,2,1,0:T(8,128)(2,1)}), bf16[32,1,24,1536]{3,2,1,0:T(8,128)(2,1)}, u32[]{:S(2)}, u32[]{:S(2)}) async-start(bf16[32,1,24,1536]{3,2,1,0:T(8,128)(2,1)} %bitcast.61), calls=%async_computation.3 | async-start | bytes 4718592 | tf_op jit(solution)/shard_map/all_to_all | solution.py:169
Sparse Core Ops, SparseCore 0:
  10.6 50.3 all-gather.2
  67.3 43.2 all-gather.4
  160.8 90.5 reduce-scatter.1
where the time goes:
time: 421 us; the launch traced here: 419 us
  waiting for transfers between devices  218 us (52%)
  blocking collectives  63.9 us (15%)
  local copies, waits for them, and re-layouts  48.4 us (11%)
  matrix products  34.3 us (8%)
  other arithmetic  21.2 us (5%)
  starting transfers between devices  16.5 us (4%)
  between operations  14 us (3%)
    reduce_scatter x1, waiting for transfers between devices, body(): lax.psum_scatter(jnp.dot(rows, w_out, preferred_element_type=jnp.float32)...  87.9 us
    all_to_all x1, blocking collectives, body(): lax.all_to_all(outgoing.reshape(group_count, local_experts, CAP, width),...  63.9 us
    all_to_all x1, waiting for transfers between devices, body(): lax.all_to_all(jnp.stack(results, axis=1), ('seq', 'tp'), split_axis=0, c...  53.2 us
    all_gather x1, waiting for transfers between devices, body(): gathered = lax.all_gather(local_keys, 'seq', axis=0, tiled=True)  41.3 us
    all_gather x1, waiting for transfers between devices, body(): lax.all_gather(normed, 'tp', axis=0, tiled=True)  26.8 us
    dot_general x5, matrix products, attend(): jnp.dot(weights.astype(jnp.bfloat16), block[:, head_dim:], preferred_elem...  14.1 us
    all_to_all x1, starting transfers between devices, body(): lax.all_to_all(own_pages, 'rep', split_axis=0, concat_axis=2, tiled=True)  11.5 us
  transfers between devices with their start and end apart: 5, of which 5 were waited for; matrix products, arithmetic and copies ran while one was open for 2% of the time, Pallas kernels for 0%

commit v1 on v0

--- a/solution.py
+++ b/solution.py
@@ -113,7 +113,21 @@
         return lax.cond(source <= seq_index, with_fresh, lambda inner: inner, state)
 
     state = start_state
-    gathered = lax.all_gather(local_keys, "seq", axis=0, tiled=True)
+    ways, here, hop = (lax.axis_size("seq"), lax.axis_index("seq"), local_keys.shape[0])
+    shape = [n * ways if d == 0 else n for d, n in enumerate(local_keys.shape)]
+    full = lax.dynamic_update_slice_in_dim(
+        jnp.zeros(shape, local_keys.dtype), local_keys, here * hop, axis=0
+    )
+    going_up = going_down = local_keys
+    for far in range(1, ways // 2 + 1):
+        going_up = lax.ppermute(going_up, "seq", [(d, (d + 1) % ways) for d in range(ways)])
+        full = lax.dynamic_update_slice_in_dim(full, going_up, (here - far) % ways * hop, axis=0)
+        if 2 * far < ways:
+            going_down = lax.ppermute(going_down, "seq", [(d, (d - 1) % ways) for d in range(ways)])
+            full = lax.dynamic_update_slice_in_dim(
+                full, going_down, (here + far) % ways * hop, axis=0
+            )
+    gathered = full
     count = gathered.shape[0] // shard_rows
     shards = gathered.reshape(count, shard_rows, pair_cols)
 

time: 421 us -> 414 us (0.983)
  waiting for transfers between devices: 218 us -> 200 us
  local copies, waits for them, and re-layouts: 48.4 us -> 56.6 us
    all_gather x1 -> x0, waiting for transfers between devices: 41.3 us -> none  [body(): gathered = lax.all_gather(local_keys, 'seq', axis=0, tiled=True)]
    ppermute x0 -> x3, waiting for transfers between devices: none -> 19.8 us  [the longest x2 19.8 us: body(): lax.ppermute(going_up, 'seq', [(d, (d + 1) % ways) for d in range(ways)])]
    unnamed x21 -> x22, local copies, waits for them, and re-layouts: 7.26 us -> 1.92 us
    ppermute x0 -> x3, local copies, waits for them, and re-layouts: none -> 5.15 us  [the longest x2 3.75 us: body(): lax.ppermute(going_up, 'seq', [(d, (d + 1) % ways) for d in range(ways)])]
    dynamic_update_slice x0 -> x4, local copies, waits for them, and re-layouts: none -> 4.92 us  [the longest x2 3.03 us: body(): lax.dynamic_update_slice_in_dim(full, going_up, (here - far) % ways * hop...]
  transfers between devices with their start and end apart: 5 -> 7, of which waited for: 5 -> 6; matrix products, arithmetic and copies ran while one was open for 2% -> 5% of each run, Pallas kernels for 0% -> 0%
where the time goes in v1:
time: 414 us; the launch traced here: 412 us
  waiting for transfers between devices  200 us (48%)
  blocking collectives  63.9 us (15%)
  local copies, waits for them, and re-layouts  56.6 us (14%)
  matrix products  34.2 us (8%)
  other arithmetic  20.1 us (5%)
  starting transfers between devices  19.5 us (5%)
  between operations  14.3 us (3%)
    reduce_scatter x1, waiting for transfers between devices, body(): lax.psum_scatter(jnp.dot(rows, w_out, preferred_element_type=jnp.float32)...  92 us
    all_to_all x1, blocking collectives, body(): lax.all_to_all(outgoing.reshape(group_count, local_experts, CAP, width),...  63.9 us
    all_to_all x1, waiting for transfers between devices, body(): lax.all_to_all(jnp.stack(results, axis=1), ('seq', 'tp'), split_axis=0, c...  53.2 us
    all_gather x1, waiting for transfers between devices, body(): lax.all_gather(normed, 'tp', axis=0, tiled=True)  26.1 us
    ppermute x2, waiting for transfers between devices, body(): lax.ppermute(going_up, 'seq', [(d, (d + 1) % ways) for d in range(ways)])  19.8 us
    dot_general x5, matrix products, attend(): jnp.dot(weights.astype(jnp.bfloat16), block[:, head_dim:], preferred_elem...  14.1 us
    all_to_all x1, starting transfers between devices, body(): lax.all_to_all(own_pages, 'rep', split_axis=0, concat_axis=2, tiled=True)  11.5 us
    all_to_all x1, waiting for transfers between devices, body(): lax.all_to_all(own_pages, 'rep', split_axis=0, concat_axis=2, tiled=True)  9.09 us
  transfers between devices with their start and end apart: 7, of which 6 were waited for; matrix products, arithmetic and copies ran while one was open for 5% of the time, Pallas kernels for 0%

profile of v1, /device:TPU:1, one launch (start us, length us, event | category | flops | bytes accessed | tf_op | source)
XLA Modules:
  0.0 412.4 jit_solution(2827620236190262105)
XLA Ops:
  12.2 11.5 %all-to-all-start = ((bf16[8,1,64,256]{3,2,1,0:T(8,128)(2,1)}), bf16[8,1,64,256]{3,2,1,0:T(8,128)(2,1)S(1)}, u32[]{:S(2)}, u32[]{:S(2)}) async-start(bf16[8,1,64,256]{3,2,1,0:T(8,128)(2,1)} %constant_dynamic-slice_fusion.2), calls=%async_computation | async-start | bytes 524288 | tf_op jit(solution)/shard_map/all_to_all | solution.py:81
  24.9 9.1 %all-to-all-done = bf16[8,1,64,256]{3,2,1,0:T(8,128)(2,1)S(1)} async-done(((bf16[8,1,64,256]{3,2,1,0:T(8,128)(2,1)}), bf16[8,1,64,256]{3,2,1,0:T(8,128)(2,1)S(1)}, u32[]{:S(2)}, u32[]{:S(2)}) %all-to-all-start) | async-done | bytes 262176 | tf_op jit(solution)/shard_map/all_to_all | solution.py:81
  34.9 26.1 %all-gather.2.cloned.1.call-done = bf16[1024,1536]{1,0:T(8,128)(2,1)} async-done(((bf16[128,1536]{1,0:T(8,128)(2,1)}), bf16[1024,1536]{1,0:T(8,128)(2,1)}) %all-gather.2.cloned.1.call-update) | async-done | bytes 3145744 | tf_op jit(solution)/shard_map/all_gather | solution.py:73
  61.0 3.4 convolution_convert_fusion.1
  67.6 16.0 %collective-permute-done = bf16[1536,256]{0,1:T(8,128)(2,1)} collective-permute-done((bf16[1536,256]{0,1:T(8,128)(2,1)S(1)}, bf16[1536,256]{0,1:T(8,128)(2,1)}, u32[]{:S(2)}, u32[]{:S(2)}) %collective-permute-start) | collective-permute-done | bytes 786464 | tf_op jit(solution)/shard_map/ppermute | solution.py:123
  97.9 3.8 collective-permute-done.2
  104.9 40.1 %while.20 = (s32[]{:T(128)}, f32[1024]{0:T(1024)S(1)}, f32[1024]{0:T(1024)S(1)}, f32[1024,128]{1,0:T(8,128)}, s32[4]{0:T(128)S(1)}, /*index=5*/s32[]{:T(128)}, s...) while((s32[]{:T(128)}, f32[1024]{0:T(1024)S(1)}, ...), condition=%wide.region_8.9_spmd.clone.clone, body=%wide.region_1.8_spmd.clone.clone.sunk | while | flops 829438464 | bytes 24546592 | solution.py:138
  108.8 2.7 convolution_add_fusion.2
  113.4 6.3 %conditional.4 = ((f32[1024]{0:T(1024)S(1)}, f32[1024]{0:T(1024)S(1)}, f32[1024,128]{1,0:T(8,128)})) conditional(s32[]{:T(128)} %convert_element_type.129, (f32[1024]{0:T(1024)S(1)}, f32[1024]{0:T(1024)S(1)}, f32[1024,128]{1,0:T(8,128)}) %tuple.70, (s32[]{:T(128)}, s32[]{:T(128)}, bf16[1,1536,256]{2,1,0:T(8,128)(2,1)S(1)}, ...), branch_computations={%region_4.4_spmd, %region_5.7_spmd} | conditional | flops 553914368 | bytes 14516288 | solution.py:113
  116.4 3.3 fusion.13
  123.5 2.7 convolution_add_fusion.2
  132.0 2.7 convolution_add_fusion.2
  145.1 4.9 %fusion.65 = f32[1024,1536]{1,0:T(8,128)} fusion(bf16[128,1536]{1,0:T(8,128)(2,1)} %param.23, f32[1024,128]{1,0:T(8,128)} %get-tuple-element.277, f32[1024]{0:T(1024)S(1)} %get-tuple-element.278), kind=kOutput, calls=%fused_computation.89 | convolution fusion | flops 402915328 | bytes 7213056 | tf_op jit(solution)/shard_map/dot_general | solution.py:143
  152.7 92.0 %reduce-scatter.2.cloned.1.call-done = f32[128,1536]{1,0:T(8,128)} async-done(((f32[1024,1536]{1,0:T(8,128)}), f32[128,1536]{1,0:T(8,128)}) %reduce-scatter.2.cloned.1.call-update) | async-done | bytes 786448 | tf_op jit(solution)/shard_map/reduce_scatter | solution.py:142
  247.8 3.7 reshape.208
  251.5 5.5 %scatter_custom_fusion = bf16[768,1536]{1,0:T(8,128)(2,1)} fusion(s32[512]{0:T(512)S(1)} %bitcast.62, bf16[512,1536]{1,0:T(8,128)(2,1)} %reshape.208, bf16[]{:T(256)} %constant.216.clone.1), kind=kCustom, calls=%fused_computation.76 | custom fusion | bytes 2359808 | tf_op jit(solution)/shard_map/scatter | solution.py:166
  257.1 63.9 %all_to_all.19 = bf16[32,1,24,1536]{3,2,1,0:T(8,128)(2,1)S(1)} all-to-all(bf16[32,1,24,1536]{3,2,1,0:T(8,128)(2,1)} %bitcast.58), channel_id=1, replica_groups=mesh['rep'=8,'seq'=4,'tp'=8] {'seq','tp'}, dimensions={0} | all-to-all | bytes 4718592 | tf_op jit(solution)/shard_map/all_to_all | solution.py:171
  321.0 5.7 %fusion.46 = f32[768,1536]{1,0:T(8,128)S(1)} fusion(bf16[768,1536]{1,0:T(8,128)(2,1)S(1)} %bitcast.60, bf16[1,1536,1536]{2,1,0:T(8,128)(2,1)} %param.26), kind=kOutput, calls=%fused_computation.57 | convolution fusion | flops 3623878656 | bytes 11796480 | tf_op jit(solution)/shard_map/dot_general | solution.py:179
  326.7 3.4 convolution_convert_fusion
  330.0 4.7 %all-to-all-start.2 = ((bf16[32,1,24,1536]{3,2,1,0:T(8,128)(2,1)}), bf16[32,1,24,1536]{3,2,1,0:T(8,128)(2,1)}, u32[]{:S(2)}, u32[]{:S(2)}) async-start(bf16[32,1,24,1536]{3,2,1,0:T(8,128)(2,1)} %bitcast.59), calls=%async_computation.3 | async-start | bytes 4718592 | tf_op jit(solution)/shard_map/all_to_all | solution.py:183
  336.8 53.2 %all-to-all-done.2 = bf16[32,1,24,1536]{3,2,1,0:T(8,128)(2,1)} async-done(((bf16[32,1,24,1536]{3,2,1,0:T(8,128)(2,1)}), bf16[32,1,24,1536]{3,2,1,0:T(8,128)(2,1)}, u32[]{:S(2)}, u32[]{:S(2)}) %all-to-all-start.2) | async-done | bytes 2359328 | tf_op jit(solution)/shard_map/all_to_all | solution.py:183
  390.0 6.4 %gather_fusion = bf16[512,1536]{1,0:T(8,128)(2,1)} fusion(bf16[768,1536]{1,0:T(8,128)(2,1)} %bitcast.14, s32[1024]{0:T(1024)S(1)} %pad_clamp_fusion), kind=kCustom, calls=%fused_computation | custom fusion | bytes 3147776 | tf_op jit(solution)/shard_map/gather | solution.py:186
  396.4 4.2 %reshape.195 = f32[128,4,1536]{2,1,0:T(4,128)} reshape(bf16[512,1536]{1,0:T(8,128)(2,1)} %gather_fusion) | data formatting | bytes 4718592 | tf_op jit(solution)/shard_map/convert_element_type | solution.py:187
  400.6 4.2 %multiply_reduce_fusion = f32[128,1536]{1,0:T(8,128)S(1)} fusion(f32[128,4,1536]{2,1,0:T(4,128)} %reshape.195, f32[128,4]{1,0:T(8,128)S(1)} %copy.54), kind=kLoop, calls=%fused_computation.60 | loop fusion | flops 1376256 | bytes 3934208 | tf_op jit(solution)/shard_map/reduce_sum | solution.py:187
  (127 shorter events, 61.6 us)
Async XLA Ops:
  7.2 319.5 %copy-start = (bf16[1,768,1536]{2,1,0:T(8,128)(2,1)S(1)}, bf16[1,768,1536]{2,1,0:T(8,128)(2,1)}, u32[]{:S(2)}) copy-start(bf16[1,768,1536]{2,1,0:T(8,128)(2,1)} %param.27) | copy-start | bytes 7077892
  7.2 53.8 %all-gather.2.cloned.1.call-start = ((), (), s32[]{:S(2)}) async-start(), calls=%async_computation.4 | async-start | bytes 3538944 | tf_op jit(solution)/shard_map/all_gather | solution.py:73
  12.2 21.8 %all-to-all-start = ((bf16[8,1,64,256]{3,2,1,0:T(8,128)(2,1)}), bf16[8,1,64,256]{3,2,1,0:T(8,128)(2,1)S(1)}, u32[]{:S(2)}, u32[]{:S(2)}) async-start(bf16[8,1,64,256]{3,2,1,0:T(8,128)(2,1)} %constant_dynamic-slice_fusion.2), calls=%async_computation | async-start | bytes 524288 | tf_op jit(solution)/shard_map/all_to_all | solution.py:81
  23.7 221.1 %reduce-scatter.2.cloned.1.call-start = ((), (), s32[]{:S(2)}) async-start(), calls=%async_computation.5 | async-start | bytes 7077888 | tf_op jit(solution)/shard_map/reduce_scatter | solution.py:142
  34.9 29.5 %copy-start.4 = (bf16[512,256]{0,1:T(8,128)(2,1)S(1)}, bf16[512,256]{0,1:T(8,128)(2,1)}, u32[]{:S(2)}) copy-start(bf16[512,256]{0,1:T(8,128)(2,1)} %copy.48) | copy-start | bytes 786436
  64.3 19.3 %copy-start.5 = (bf16[1024,384]{0,1:T(8,128)(2,1)}, bf16[1024,384]{0,1:T(8,128)(2,1)S(1)}, u32[]{:S(2)}) copy-start(bf16[1024,384]{0,1:T(8,128)(2,1)S(1)} %convolution_convert_fusion.1) | copy-start | bytes 2359300
  64.3 19.4 %copy-start.9 = (s32[8]{0:T(128)S(1)}, s32[8]{0:T(128)}, u32[]{:S(2)}) copy-start(s32[8]{0:T(128)} %param.18) | copy-start | bytes 100
  64.4 19.2 %copy-start.3 = (bf16[1024,256]{0,1:T(8,128)(2,1)}, bf16[1024,256]{0,1:T(8,128)(2,1)S(1)}, u32[]{:S(2)}) copy-start(bf16[1024,256]{0,1:T(8,128)(2,1)S(1)} %slice.74) | copy-start | bytes 1572868
  64.5 19.2 %collective-permute-start = (bf16[1536,256]{0,1:T(8,128)(2,1)S(1)}, bf16[1536,256]{0,1:T(8,128)(2,1)}, u32[]{:S(2)}, u32[]{:S(2)}) collective-permute-start(bf16[1536,256]{0,1:T(8,128)(2,1)S(1)} %pad_maximum_fusion), channel_id=1, source_target_pairs={{0,8},{8,16},{16,24},{24,0},{1,9},{9,17},{17,25},{25,1},{2,10},{10... | collective-permute-start | bytes 2359304 | tf_op jit(solution)/shard_map/ppermute | solution.py:123
  66.1 27.4 %collective-permute-start.1 = (bf16[1536,256]{0,1:T(8,128)(2,1)S(1)}, bf16[1536,256]{0,1:T(8,128)(2,1)}, u32[]{:S(2)}, u32[]{:S(2)}) collective-permute-start(bf16[1536,256]{0,1:T(8,128)(2,1)S(1)} %pad_maximum_fusion), channel_id=1, source_target_pairs={{0,24},{8,0},{16,8},{24,16},{1,25},{9,1},{17,9},{25,17},{2,26},{10... | collective-permute-start | bytes 2359304 | tf_op jit(solution)/shard_map/ppermute | solution.py:126
  83.6 18.1 %collective-permute-start.2 = (bf16[1536,256]{0,1:T(8,128)(2,1)}, bf16[1536,256]{0,1:T(8,128)(2,1)}, u32[]{:S(2)}, u32[]{:S(2)}) collective-permute-start(bf16[1536,256]{0,1:T(8,128)(2,1)} %collective-permute-done), channel_id=1, source_target_pairs={{0,8},{8,16},{16,24},{24,0},{1,9},{9,17},{17,25},{25,1},{2,10},{10... | collective-permute-start | bytes 2359304 | tf_op jit(solution)/shard_map/ppermute | solution.py:123
  88.3 1.9 copy-start.2
  149.9 0.7 copy-start.7
  149.9 94.8 %copy-start.1 = (bf16[128,1536]{1,0:T(8,128)(2,1)S(1)}, bf16[128,1536]{1,0:T(8,128)(2,1)}, u32[]{:S(2)}) copy-start(bf16[128,1536]{1,0:T(8,128)(2,1)} %param.16) | copy-start | bytes 1179652
  149.9 96.2 %copy-start.8 = (f32[1536]{0:T(1024)S(1)}, f32[1536]{0:T(1024)}, u32[]{:S(2)}) copy-start(f32[1536]{0:T(1024)} %param.24) | copy-start | bytes 18436
  330.0 6.3 %copy-start.6 = (bf16[1536,32]{0,1:T(8,128)(2,1)S(1)}, bf16[1536,32]{0,1:T(8,128)(2,1)}, u32[]{:S(2)}) copy-start(bf16[1536,32]{0,1:T(8,128)(2,1)} %param.25) | copy-start | bytes 294916
  330.0 60.0 %all-to-all-start.2 = ((bf16[32,1,24,1536]{3,2,1,0:T(8,128)(2,1)}), bf16[32,1,24,1536]{3,2,1,0:T(8,128)(2,1)}, u32[]{:S(2)}, u32[]{:S(2)}) async-start(bf16[32,1,24,1536]{3,2,1,0:T(8,128)(2,1)} %bitcast.59), calls=%async_computation.3 | async-start | bytes 4718592 | tf_op jit(solution)/shard_map/all_to_all | solution.py:183
Sparse Core Ops, SparseCore 0:
  10.6 50.3 all-gather.1
  150.1 94.6 reduce-scatter.1
